TPU v7x, 256 devices: a whole 4x4x8 slice. The times are simulated.
256 devices in a mesh: context: 64 (over y, x_lo, z), heads: 4 (over x_hi, core).
Axes of the slice: x: 4 (x_hi: 2, x_lo: 2; x = x_hi * 2 + x_lo), y: 4, z: 8, core: 2. Of those that a mesh axis runs over, the one named last changes fastest.
Arguments:
- upstream: bfloat16 [16384, 1024], P(('context', 'heads')), may hold values from -48 to 48
- out_weight: bfloat16 [1024, 1024], P('heads'), may hold values from -0.1875 to 0.1875
- query_rows: bfloat16 [16384, 1024], P('context', 'heads'), may hold values from -6 to 6
- key_rows: bfloat16 [16384, 1024], P('context', 'heads'), may hold values from -6 to 6
- value_rows: bfloat16 [16384, 1024], P('context', 'heads'), may hold values from -6 to 6
- head_offsets: int32 [16], replicated, may hold values from 0 to 15, each once
Outputs:
- query_grad: bfloat16 [16384, 1024], P('context', 'heads')
- key_grad: bfloat16 [16384, 1024], P('context', 'heads')
- value_grad: bfloat16 [16384, 1024], P('context', 'heads')
Inputs may be any that keep to these rules, and one draw needn't show every extreme that they name: `head_offsets`: every value of 0 to 15 occurs once.
All inputs are finite; a program needn't handle non-finite values.
Results may differ from a plain program's by a relative error of at most 0.008.
Values may be sent and summed in bfloat16 or wider, within the bound.
A program may use at most 128 MiB of HBM per device.

v0:
```python
import math
import jax
import jax.numpy as jnp
from jax import lax
from jax.sharding import PartitionSpec as P

HEAD_SIZE = 64
DILATION_RATE = 16
FIRST_SEGMENT = 2048


def partner_2(value, axis, apart):
    mask = 2**apart
    pairs = [(source, source ^ mask) for source in range(lax.axis_size(axis))]
    return lax.ppermute(value, axis, pairs)


def dot_rows(left, right):
    return lax.dot_general(
        left, right, (((1,), (1,)), ((), ())), preferred_element_type=jnp.float32
    )


def dot_cols(left, right):
    return lax.dot_general(
        left, right, (((0,), (0,)), ((), ())), preferred_element_type=jnp.float32
    )


def pick_rows(payload_arrays, mask_stack):
    span_length, block_width = payload_arrays.shape
    head_count = mask_stack.shape[1]
    launch_layout = payload_arrays.reshape(
        span_length // DILATION_RATE, DILATION_RATE, head_count, block_width // head_count
    )
    selected_rows = jnp.where(
        mask_stack[None, :, :, None], launch_layout, jnp.zeros((), payload_arrays.dtype)
    )
    return jnp.sum(selected_rows, axis=1).reshape(span_length // DILATION_RATE, block_width)


def place_rows(picked, mask_stack):
    total_count, block_width = picked.shape
    head_count = mask_stack.shape[1]
    launch_layout = picked.reshape(total_count, 1, head_count, block_width // head_count)
    dispersal_rows = jnp.where(
        mask_stack[None, :, :, None], launch_layout, jnp.zeros((), picked.dtype)
    )
    return dispersal_rows.reshape(total_count * DILATION_RATE, block_width)


def spread_rows(value_tensor, head_shift):
    total_count = value_tensor.shape[0]
    matched_flag = jnp.arange(DILATION_RATE, dtype=jnp.int32)[None, :] == head_shift
    return jnp.where(
        matched_flag, value_tensor[:, None], jnp.zeros((), value_tensor.dtype)
    ).reshape(total_count * DILATION_RATE)


def double_up(buffer, levels, position):
    for level in range(levels):
        partner = partner_2(buffer, "context", level)
        lower = position >> level & 1 == 0
        buffer = jnp.where(
            lower, jnp.concatenate([buffer, partner], 1), jnp.concatenate([partner, buffer], 1)
        )
    return buffer


def halve_down(buffer, levels, position):
    for level in range(levels - 1, -1, -1):
        middle = buffer.shape[1] // 2
        lower_half = buffer[:, :middle]
        upper_half = buffer[:, middle:]
        lower = position >> level & 1 == 0
        kept = jnp.where(lower, lower_half, upper_half)
        outgoing = jnp.where(lower, upper_half, lower_half)
        incoming = partner_2(outgoing, "context", level)
        buffer = kept + incoming
    return buffer


def body(upstream, out_weight, query_rows, key_rows, value_rows, head_offsets):
    position = lax.axis_index("context")
    span_length, block_width = query_rows.shape
    head_count = block_width // HEAD_SIZE
    scale = 1.0 / math.sqrt(HEAD_SIZE)
    partial_rows = dot_rows(upstream, lax.all_gather(out_weight, "heads", axis=0, tiled=True))
    attn_grad = lax.all_to_all(
        partial_rows.astype(jnp.bfloat16), "heads", split_axis=1, concat_axis=0, tiled=True
    )
    local_shifts = lax.dynamic_slice_in_dim(
        head_offsets, lax.axis_index("heads") * head_count, head_count
    )
    mask_stack = jnp.arange(DILATION_RATE, dtype=jnp.int32)[:, None] == local_shifts[None, :]
    query_pick = pick_rows(query_rows, mask_stack)
    grad_pick = pick_rows(attn_grad, mask_stack)
    key_pick = pick_rows(key_rows, mask_stack)
    value_pick = pick_rows(value_rows, mask_stack)
    picked_pair = jnp.stack([key_pick, value_pick])
    dense_span = FIRST_SEGMENT // span_length
    dense_levels = dense_span.bit_length() - 1
    near_pair = double_up(jnp.stack([key_rows, value_rows]), dense_levels, position)
    far_pair = lax.all_gather(picked_pair, "context", axis=1, tiled=True)
    block_rows = min(512, span_length)
    num_blocks = span_length // block_rows
    current_row_index = jnp.arange(span_length, dtype=jnp.int32)
    dq_near_list, dk_near_list, dv_near_list = ([], [], [])
    dq_far_list, dk_far_list, dv_far_list = ([], [], [])
    lse_list, delta_list = ([], [])
    for head in range(head_count):
        columns = slice(head * HEAD_SIZE, (head + 1) * HEAD_SIZE)
        head_shift = local_shifts[head]
        query_head = query_rows[:, columns]
        grad_head = attn_grad[:, columns]
        near_keys = near_pair[0][:, columns]
        near_values = near_pair[1][:, columns]
        query_sel = query_pick[:, columns]
        grad_sel = grad_pick[:, columns]
        far_keys = far_pair[0][:, columns]
        far_values = far_pair[1][:, columns]
        score_near = dot_rows(query_sel, near_keys) * scale
        score_far = dot_rows(query_sel, far_keys) * scale
        row_max = jnp.maximum(jnp.max(score_near, 1), jnp.max(score_far, 1))
        row_sum = jnp.sum(jnp.exp(score_near - row_max[:, None]), 1) + jnp.sum(
            jnp.exp(score_far - row_max[:, None]), 1
        )
        lse_sel = row_max + jnp.log(row_sum)
        prob_near = jnp.exp(score_near - lse_sel[:, None])
        prob_far = jnp.exp(score_far - lse_sel[:, None])
        dprob_near = dot_rows(grad_sel, near_values)
        dprob_far = dot_rows(grad_sel, far_values)
        delta_sel = jnp.sum(prob_near * dprob_near, 1) + jnp.sum(prob_far * dprob_far, 1)
        dscore_far = (prob_far * (dprob_far - delta_sel[:, None])).astype(jnp.bfloat16)
        dq_far_list.append(
            jnp.dot(dscore_far, far_keys, preferred_element_type=jnp.float32) * scale
        )
        lse_list.append(lse_sel)
        delta_list.append(delta_sel)
        prob_far16 = prob_far.astype(jnp.bfloat16)
        dk_far_list.append(dot_cols(dscore_far, query_sel) * scale)
        dv_far_list.append(dot_cols(prob_far16, grad_sel))
        lse_rows = spread_rows(lse_sel, head_shift)
        delta_rows = spread_rows(delta_sel, head_shift)
        selected_rows = current_row_index % DILATION_RATE == head_shift

        def step(carry, inputs):
            key_acc, value_acc = carry
            query_blk, grad_blk, lse_blk, delta_blk, mask_blk = inputs
            scores = dot_rows(query_blk, near_keys) * scale
            blk_max = jnp.max(scores, 1)
            blk_sum = jnp.sum(jnp.exp(scores - blk_max[:, None]), 1)
            lse_all = jnp.where(mask_blk, lse_blk, blk_max + jnp.log(blk_sum))
            probs = jnp.exp(scores - lse_all[:, None])
            dprobs = dot_rows(grad_blk, near_values)
            delta_all = jnp.where(mask_blk, delta_blk, jnp.sum(probs * dprobs, 1))
            dscores = (probs * (dprobs - delta_all[:, None])).astype(jnp.bfloat16)
            probs16 = probs.astype(jnp.bfloat16)
            dq_blk = jnp.dot(dscores, near_keys, preferred_element_type=jnp.float32) * scale
            key_acc = key_acc + dot_cols(dscores, query_blk) * scale
            value_acc = value_acc + dot_cols(probs16, grad_blk)
            return ((key_acc, value_acc), dq_blk)

        zeros_acc = jnp.zeros((near_keys.shape[0], HEAD_SIZE), jnp.float32)
        (key_acc, value_acc), dq_blocks = lax.scan(
            step,
            (zeros_acc, zeros_acc),
            (
                query_head.reshape(num_blocks, block_rows, HEAD_SIZE),
                grad_head.reshape(num_blocks, block_rows, HEAD_SIZE),
                lse_rows.reshape(num_blocks, block_rows),
                delta_rows.reshape(num_blocks, block_rows),
                selected_rows.reshape(num_blocks, block_rows),
            ),
        )
        dq_near_list.append(dq_blocks.reshape(span_length, HEAD_SIZE))
        dk_near_list.append(key_acc)
        dv_near_list.append(value_acc)
    near_terms = jnp.stack([jnp.concatenate(dk_near_list, 1), jnp.concatenate(dv_near_list, 1)])
    near_back = halve_down(near_terms, dense_levels, position)
    far_terms = jnp.stack([jnp.concatenate(dk_far_list, 1), jnp.concatenate(dv_far_list, 1)])
    far_back = lax.psum_scatter(far_terms, "context", scatter_dimension=1, tiled=True)
    far_key_grad = far_back[0]
    far_value_grad = far_back[1]
    query_grad = (
        jnp.concatenate(dq_near_list, 1) + place_rows(jnp.concatenate(dq_far_list, 1), mask_stack)
    ).astype(jnp.bfloat16)
    key_grad = (near_back[0] + place_rows(far_key_grad, mask_stack)).astype(jnp.bfloat16)
    value_grad = (near_back[1] + place_rows(far_value_grad, mask_stack)).astype(jnp.bfloat16)
    return (query_grad, key_grad, value_grad)


def solution(mesh):
    return jax.shard_map(
        body,
        mesh=mesh,
        in_specs=(
            P(("context", "heads"), None),
            P("heads", None),
            P("context", "heads"),
            P("context", "heads"),
            P("context", "heads"),
            P(),
        ),
        out_specs=(P("context", "heads"), P("context", "heads"), P("context", "heads")),
        check_vma=False,
    )
```

profile of v0, /device:TPU:4, one launch (start us, length us, event | category | flops | bytes accessed | tf_op | source)
XLA Modules:
  0.0 1150.2 jit_solution(13889192455797140097)
XLA Ops:
  8.3 2.0 collective-permute-start
  10.4 6.2 collective-permute-done
  16.6 1.3 maximum_select_fusion.2
  17.9 3.4 collective-permute-start.1
  21.2 22.5 %collective-permute-done.1 = bf16[2,512,256]{2,1,0:T(8,128)(2,1)S(1)} collective-permute-done((bf16[2,512,256]{2,1,0:T(8,128)(2,1)S(1)}, bf16[2,512,256]{2,1,0:T(8,128)(2,1)S(1)}, u32[]{:S(2)}, u32[]{:S(2)}) %collective-permute-start.1) | collective-permute-done | bytes 524320 | tf_op jit(solution)/shard_map/ppermute | solution.py:15
  44.0 6.3 collective-permute-start.2
  54.9 1.2 iota_compare_fusion.4
  56.0 1.1 iota_compare_fusion.1
  58.2 1.2 iota_compare_fusion.3
  59.5 36.6 %collective-permute-done.2 = bf16[2,1024,256]{2,1,0:T(8,128)(2,1)S(1)} collective-permute-done((bf16[2,1024,256]{2,1,0:T(8,128)(2,1)S(1)}, bf16[2,1024,256]{2,1,0:T(8,128)(2,1)S(1)}, u32[]{:S(2)}, u32[]{:S(2)}) %collective-permute-start.2) | collective-permute-done | bytes 1048608 | tf_op jit(solution)/shard_map/ppermute | solution.py:15
  96.5 1.2 slice_bitcast_fusion.1
  97.7 1.9 fusion.135
  100.2 2.3 convolution_convert_fusion
  103.2 4.8 all-to-all-start
  108.0 2.5 exponential_reduce_fusion
  111.8 2.0 select_reduce_fusion.3
  116.4 1.3 copy-done.6
  119.2 1.3 copy-done.3
  121.6 1.6 fusion.133
  123.2 1.6 fusion.131
  124.8 1.6 fusion.129
  126.4 1.6 fusion.127
  128.0 284.4 %all-gather.3.cloned.1.call-done = bf16[2,1024,256]{2,1,0:T(8,128)(2,1)} async-done(((bf16[2,16,256]{2,1,0:T(8,128)(2,1)}), bf16[2,1024,256]{2,1,0:T(8,128)(2,1)}) %all-gather.3.cloned.1.call-update) | async-done | bytes 1048592 | tf_op jit(solution)/shard_map/all_gather | solution.py:104
  412.4 1.4 slice_bitcast_fusion.3
  417.2 1.8 fusion.9
  419.0 1.4 multiply_reduce_fusion.3
  421.9 1.6 multiply_reduce_fusion.2
  424.9 1.5 multiply_reduce_fusion.1
  430.0 1.3 select_n.327
  431.3 1.5 add_select_fusion
  432.8 2.9 fusion.16
  435.7 3.5 fusion.1
  440.0 1.3 select_n.321
  441.3 1.3 add_select_fusion.1
  442.5 1.3 fusion.15
  443.8 2.4 fusion.3
  447.0 1.4 select_n.315
  448.4 1.5 add_select_fusion.2
  449.8 2.9 fusion.14
  452.8 3.6 fusion.5
  457.1 1.4 select_n.308
  458.4 1.5 add_select_fusion.3
  459.9 2.8 fusion.13
  462.8 3.5 fusion.7
  466.4 1.3 select_n.312
  468.7 1.3 select_n.318
  470.9 1.4 select_n.324
  473.3 1.4 select_n.330
  475.5 1.3 fusion.125
  476.8 2.8 fusion.2
  481.8 1.2 fusion.123
  484.4 1.2 fusion.122
  488.3 1.9 broadcast_select_fusion
  491.6 1.6 pad_maximum_fusion.1
  493.2 4.1 copy.51
  498.4 1.2 convolution_multiply_fusion.30
  500.7 1.2 convolution_multiply_fusion.28
  501.9 51.9 %collective-permute-done.3 = f32[2,1024,256]{1,2,0:T(8,128)} collective-permute-done((f32[2,1024,256]{1,2,0:T(8,128)}, f32[2,1024,256]{1,2,0:T(8,128)}, u32[]{:S(2)}, u32[]{:S(2)}) %collective-permute-start.3) | collective-permute-done | bytes 2097184 | tf_op jit(solution)/shard_map/ppermute | solution.py:15
  553.8 2.9 select_add_fusion
  558.0 1.2 convolution_multiply_fusion.20
  560.2 1.2 convolution_multiply_fusion.24
  562.3 22.9 %collective-permute-done.4 = f32[2,512,256]{1,2,0:T(8,128)S(1)} collective-permute-done((f32[2,512,256]{1,2,0:T(8,128)S(1)}, f32[2,512,256]{1,2,0:T(8,128)S(1)}, u32[]{:S(2)}, u32[]{:S(2)}) %collective-permute-start.4) | collective-permute-done | bytes 1048608 | tf_op jit(solution)/shard_map/ppermute | solution.py:15
  586.5 2.3 collective-permute-start.5
  588.9 548.2 %all-reduce.3.cloned.1.call-done = f32[2,1024,256]{2,0,1:T(2,128)} async-done(((f32[2,1024,256]{2,0,1:T(2,128)}), f32[2,1024,256]{2,0,1:T(2,128)}) %all-reduce.3.cloned.1.call-update) | async-done | bytes 2097168
  (298 shorter events, 50.3 us)
Async XLA Ops:
  7.2 93.0 %copy-start = (bf16[64,1024]{1,0:T(8,128)(2,1)S(1)}, bf16[64,1024]{1,0:T(8,128)(2,1)}, u32[]{:S(2)}) copy-start(bf16[64,1024]{1,0:T(8,128)(2,1)} %param.6) | copy-start | bytes 393220
  7.2 93.0 %all-gather.5.cloned.1.call-start = ((), (), s32[]{:S(2)}) async-start(), calls=%async_computation.2 | async-start | bytes 2621440 | tf_op jit(solution)/shard_map/all_gather | solution.py:88
  7.2 43.0 %copy-start.35 = (bf16[256,256]{1,0:T(8,128)(2,1)S(1)}, bf16[256,256]{1,0:T(8,128)(2,1)}, u32[]{:S(2)}) copy-start(bf16[256,256]{1,0:T(8,128)(2,1)} %param.9) | copy-start | bytes 393220
  8.3 42.8 %copy-start.36 = (bf16[256,256]{1,0:T(8,128)(2,1)S(1)}, bf16[256,256]{1,0:T(8,128)(2,1)}, u32[]{:S(2)}) copy-start(bf16[256,256]{1,0:T(8,128)(2,1)} %param.10) | copy-start | bytes 393220
  8.3 8.3 collective-permute-start
  10.3 41.7 %copy-start.24 = (bf16[256,256]{1,0:T(8,128)(2,1)S(1)}, bf16[256,256]{1,0:T(8,128)(2,1)}, u32[]{:S(2)}) copy-start(bf16[256,256]{1,0:T(8,128)(2,1)} %param.8) | copy-start | bytes 393220
  10.4 42.5 %copy-start.92 = (u32[256]{0:T(256)S(1)}, u32[256]{0:T(256)}, u32[]{:S(2)}) copy-start(u32[256]{0:T(256)} %constant.137) | copy-start | bytes 3076
  10.4 43.8 %copy-start.91 = (s32[16]{0:T(128)S(1)}, s32[16]{0:T(128)}, u32[]{:S(2)}) copy-start(s32[16]{0:T(128)} %param.11) | copy-start | bytes 196
  17.9 25.8 %collective-permute-start.1 = (bf16[2,512,256]{2,1,0:T(8,128)(2,1)S(1)}, bf16[2,512,256]{2,1,0:T(8,128)(2,1)S(1)}, u32[]{:S(2)}, u32[]{:S(2)}) collective-permute-start(bf16[2,512,256]{2,1,0:T(8,128)(2,1)S(1)} %maximum_select_fusion.2), channel_id=1, source_target_pairs={{0,8},{4,12},{8,0},{12,4},{16,24},{20,28},{24,16},{28,20},{32,40},... | collective-permute-start | bytes 1572872 | tf_op jit(solution)/shard_map/ppermute | solution.py:15
  44.0 52.1 %collective-permute-start.2 = (bf16[2,1024,256]{2,1,0:T(8,128)(2,1)S(1)}, bf16[2,1024,256]{2,1,0:T(8,128)(2,1)S(1)}, u32[]{:S(2)}, u32[]{:S(2)}) collective-permute-start(bf16[2,1024,256]{2,1,0:T(8,128)(2,1)S(1)} %maximum_select_fusion.1), channel_id=1, source_target_pairs={{0,16},{4,20},{8,24},{12,28},{16,0},{20,4},{24,8},{28,12},{32,48},... | collective-permute-start | bytes 3145736 | tf_op jit(solution)/shard_map/ppermute | solution.py:15
  59.5 52.3 %copy-start.43 = (pred[16,4]{1,0:T(8,128)(4,1)}, pred[16,4]{1,0:T(8,128)(4,1)S(1)}, u32[]{:S(2)}) copy-start(pred[16,4]{1,0:T(8,128)(4,1)S(1)} %iota_compare_fusion) | copy-start | bytes 196
  99.6 8.4 copy-start.64
  100.1 14.8 %copy-start.63 = (f32[256]{0:T(256)}, f32[256]{0:T(256)S(1)}, u32[]{:S(2)}) copy-start(f32[256]{0:T(256)S(1)} %get-tuple-element.199) | copy-start | bytes 3076
  103.2 7.8 all-to-all-start
  108.0 304.4 %all-gather.3.cloned.1.call-start = ((), (), s32[]{:S(2)}) async-start(), calls=%async_computation.1 | async-start | bytes 1064960 | tf_op jit(solution)/shard_map/all_gather | solution.py:104
  114.7 1022.5 %all-reduce.3.cloned.1.call-start = ((), (), s32[]{:S(2)}) async-start(), calls=%async_computation.3 | async-start | bytes 4194304
  412.4 4.8 copy-start.9
  412.4 8.1 copy-start.90
  412.4 8.3 copy-start.34
  413.8 11.1 copy-start.12
  413.8 9.8 copy-start.89
  413.8 9.9 copy-start.33
  414.2 14.1 %copy-start.31 = (f32[16,1024]{1,0:T(8,128)}, f32[16,1024]{1,0:T(8,128)S(1)}, u32[]{:S(2)}) copy-start(f32[16,1024]{1,0:T(8,128)S(1)} %get-tuple-element.163) | copy-start | bytes 196612
  414.8 11.7 %copy-start.29 = (f32[16,1024]{1,0:T(8,128)}, f32[16,1024]{1,0:T(8,128)S(1)}, u32[]{:S(2)}) copy-start(f32[16,1024]{1,0:T(8,128)S(1)} %get-tuple-element.182) | copy-start | bytes 196612
  414.8 11.5 %copy-start.88 = (f32[16]{0:T(128)S(1)}, f32[16]{0:T(128)}, u32[]{:S(2)}) copy-start(f32[16]{0:T(128)} %get-tuple-element.160) | copy-start | bytes 196
  414.9 11.7 %copy-start.32 = (f32[16,2048]{1,0:T(8,128)S(1)}, f32[16,2048]{1,0:T(8,128)}, u32[]{:S(2)}) copy-start(f32[16,2048]{1,0:T(8,128)} %get-tuple-element.161) | copy-start | bytes 393220
  417.2 10.6 copy-start.45
  420.5 8.8 copy-start.87
  420.9 8.3 copy-start.49
  424.0 5.3 copy-start.52
  431.3 4.4 copy-start.2
  432.8 6.5 copy-start.56
  435.7 3.5 copy-start.82
  435.7 3.5 copy-start.83
  435.7 3.5 copy-start.53
  435.7 3.5 copy-start.86
  442.5 3.7 copy-start.57
  448.4 4.4 copy-start.7
  449.8 6.5 copy-start.59
  452.8 3.6 copy-start.78
  452.8 3.6 copy-start.79
  452.8 3.6 copy-start.46
  452.8 3.6 copy-start.84
  458.4 4.3 copy-start.4
  459.9 6.4 copy-start.61
  462.7 3.5 copy-start.42
  462.7 3.5 copy-start.47
  462.8 3.5 copy-start.77
  470.9 8.6 copy-start.38
  473.3 6.3 copy-start.40
  476.8 3.3 copy-start.67
  476.8 3.3 copy-start.72
  476.8 3.9 copy-start.21
  476.8 3.9 copy-start.58
  488.3 2.8 copy-start.48
  488.3 3.0 copy-start.37
  490.3 63.6 %collective-permute-start.3 = (f32[2,1024,256]{1,2,0:T(8,128)}, f32[2,1024,256]{1,2,0:T(8,128)}, u32[]{:S(2)}, u32[]{:S(2)}) collective-permute-start(f32[2,1024,256]{1,2,0:T(8,128)} %broadcast_select_fusion), channel_id=1, source_target_pairs={{0,16},{4,20},{8,24},{12,28},{16,0},{20,4},{24,8},{28,12},{32,48},... | collective-permute-start | bytes 6291464 | tf_op jit(solution)/shard_map/ppermute | solution.py:15
  497.3 3.4 copy-start.41
  557.0 3.2 copy-start.18
  557.0 4.4 copy-start.20
  557.0 28.3 %collective-permute-start.4 = (f32[2,512,256]{1,2,0:T(8,128)S(1)}, f32[2,512,256]{1,2,0:T(8,128)S(1)}, u32[]{:S(2)}, u32[]{:S(2)}) collective-permute-start(f32[2,512,256]{1,2,0:T(8,128)S(1)} %slice_select_fusion), channel_id=1, source_target_pairs={{0,8},{4,12},{8,0},{12,4},{16,24},{20,28},{24,16},{28,20},{32,40},... | collective-permute-start | bytes 3145736 | tf_op jit(solution)/shard_map/ppermute | solution.py:15
  562.3 575.9 %copy-start.44 = (pred[16,4]{1,0:T(8,128)(4,1)S(1)}, pred[16,4]{1,0:T(8,128)(4,1)}, u32[]{:S(2)}) copy-start(pred[16,4]{1,0:T(8,128)(4,1)} %copy-done.43) | copy-start | bytes 196
  586.5 555.5 %collective-permute-start.5 = (f32[2,256,256]{1,2,0:T(8,128)}, f32[2,256,256]{1,2,0:T(8,128)S(1)}, u32[]{:S(2)}, u32[]{:S(2)}) collective-permute-start(f32[2,256,256]{1,2,0:T(8,128)} %slice_select_fusion.1), channel_id=1, source_target_pairs={{0,4},{4,0},{8,12},{12,8},{16,20},{20,16},{24,28},{28,24},{32,36},... | collective-permute-start | bytes 1572872 | tf_op jit(solution)/shard_map/ppermute | solution.py:15
  1140.2 3.5 copy-start.1
  (39 other events, 72.9 us)
Sparse Core Ops, SparseCore 0:
  10.5 28.7 all-gather.4
  114.8 297.5 all-gather.2
  497.4 639.6 all-reduce.2
where the time goes:
time: 1150 us
  waiting for transfers between devices  973 us (85%)
  matrix products  60 us (5%)
  other arithmetic  48.8 us (4%)
  local copies, waits for them, and re-layouts  33.5 us (3%)
  starting transfers between devices  19.1 us (2%)
  between operations  15.5 us (1%)
    unnamed x4, waiting for transfers between devices  548 us
    all_gather x1, waiting for transfers between devices, body(): far_pair = lax.all_gather(picked_pair, 'context', axis=1, tiled=True)  284 us
    ppermute x6, waiting for transfers between devices, partner_2(): return lax.ppermute(value, axis, pairs)  140 us
    dot_general x25, matrix products, dot_rows(): lax.dot_general(left, right, (((1,), (1,)), ((), ())), preferred_element_...  36.3 us
  transfers between devices with their start and end apart: 10, of which 8 were waited for; matrix products, arithmetic and copies ran while one was open for 5% of the time, Pallas kernels for 0%

commit v1 on v0

--- a/solution.py
+++ b/solution.py
@@ -101,7 +101,9 @@
     dense_span = FIRST_SEGMENT // span_length
     dense_levels = dense_span.bit_length() - 1
     near_pair = double_up(jnp.stack([key_rows, value_rows]), dense_levels, position)
-    far_pair = lax.all_gather(picked_pair, "context", axis=1, tiled=True)
+    far_pair = jnp.concatenate(
+        lax.all_to_all(jnp.stack([picked_pair] * lax.psum(1, "context")), "context", 0, 0), 1
+    )
     block_rows = min(512, span_length)
     num_blocks = span_length // block_rows
     current_row_index = jnp.arange(span_length, dtype=jnp.int32)

time: 1150 us -> 917 us (0.80)
  waiting for transfers between devices: 973 us -> 696 us
  starting transfers between devices: 19.1 us -> 61.5 us
    all_gather x1 -> x0, waiting for transfers between devices: 284 us -> none  [body(): far_pair = lax.all_gather(picked_pair, 'context', axis=1, tiled=True)]
    ppermute x6, starting transfers between devices: 14.1 us -> 47.6 us  [partner_2(): return lax.ppermute(value, axis, pairs)]
    unnamed x4 -> x3, waiting for transfers between devices: 548 us -> 519 us
    ppermute x6, waiting for transfers between devices: 140 us -> 161 us  [partner_2(): return lax.ppermute(value, axis, pairs)]
    all_to_all x0 -> x1, waiting for transfers between devices: none -> 15.6 us  [body(): lax.all_to_all(jnp.stack([picked_pair] * lax.psum(1, 'context')), 'contex...]
  transfers between devices with their start and end apart: 10 -> 10, of which waited for: 8 -> 8; matrix products, arithmetic and copies ran while one was open for 5% -> 6% of each run, Pallas kernels for 0% -> 0%
where the time goes in v1:
time: 917 us; the launch traced here: 915 us
  waiting for transfers between devices  696 us (76%)
  starting transfers between devices  61.5 us (7%)
  matrix products  60 us (7%)
  other arithmetic  48.3 us (5%)
  local copies, waits for them, and re-layouts  33.7 us (4%)
  between operations  16 us (2%)
    unnamed x3, waiting for transfers between devices  519 us
    ppermute x6, waiting for transfers between devices, partner_2(): return lax.ppermute(value, axis, pairs)  161 us
    ppermute x6, starting transfers between devices, partner_2(): return lax.ppermute(value, axis, pairs)  47.6 us
    dot_general x25, matrix products, dot_rows(): lax.dot_general(left, right, (((1,), (1,)), ((), ())), preferred_element_...  36.3 us
  transfers between devices with their start and end apart: 10, of which 8 were waited for; matrix products, arithmetic and copies ran while one was open for 6% of the time, Pallas kernels for 0%

profile of v1, /device:TPU:4, one launch (start us, length us, event | category | flops | bytes accessed | tf_op | source)
XLA Modules:
  0.0 915.1 jit_solution(14876698733321965472)
XLA Ops:
  8.3 2.0 collective-permute-start
  10.4 6.2 collective-permute-done
  16.6 1.3 maximum_select_fusion.2
  17.9 3.4 collective-permute-start.1
  21.2 22.5 %collective-permute-done.1 = bf16[2,512,256]{2,1,0:T(8,128)(2,1)S(1)} collective-permute-done((bf16[2,512,256]{2,1,0:T(8,128)(2,1)S(1)}, bf16[2,512,256]{2,1,0:T(8,128)(2,1)S(1)}, u32[]{:S(2)}, u32[]{:S(2)}) %collective-permute-start.1) | collective-permute-done | bytes 524320 | tf_op jit(solution)/shard_map/ppermute | solution.py:15
  44.0 6.3 collective-permute-start.2
  54.8 1.2 iota_compare_fusion.4
  56.1 1.2 iota_compare_fusion.1
  58.4 1.2 iota_compare_fusion.3
  59.5 36.5 %collective-permute-done.2 = bf16[2,1024,256]{2,1,0:T(8,128)(2,1)S(1)} collective-permute-done((bf16[2,1024,256]{2,1,0:T(8,128)(2,1)S(1)}, bf16[2,1024,256]{2,1,0:T(8,128)(2,1)S(1)}, u32[]{:S(2)}, u32[]{:S(2)}) %collective-permute-start.2) | collective-permute-done | bytes 1048608 | tf_op jit(solution)/shard_map/ppermute | solution.py:15
  97.7 1.9 fusion.136
  100.2 2.3 convolution_convert_fusion
  103.2 4.8 all-to-all-start.1
  108.0 2.5 exponential_reduce_fusion
  111.8 2.0 select_reduce_fusion.3
  115.2 8.9 all-to-all-start
  125.7 1.3 copy-done.6
  128.6 1.3 copy-done.3
  131.0 1.5 fusion.134
  132.6 1.6 fusion.132
  134.1 1.6 fusion.130
  135.7 1.6 fusion.128
  137.3 15.6 %all-to-all-done = bf16[64,2,16,256]{3,2,1,0:T(8,128)(2,1)} async-done(((bf16[64,2,16,256]{3,2,1,0:T(8,128)(2,1)}), bf16[64,2,16,256]{3,2,1,0:T(8,128)(2,1)}, u32[]{:S(2)}, u32[]{:S(2)}) %all-to-all-start) | async-done | bytes 1048608 | tf_op jit(solution)/shard_map/all_to_all | solution.py:105
  153.0 1.4 fusion.126
  157.7 1.9 fusion.9
  159.6 1.5 multiply_reduce_fusion.3
  162.6 1.5 multiply_reduce_fusion.2
  165.5 1.5 multiply_reduce_fusion.1
  170.6 1.3 select_n.327
  171.9 1.5 add_select_fusion
  173.4 3.0 fusion.16
  176.4 3.5 fusion.1
  180.6 1.3 select_n.321
  181.9 1.4 add_select_fusion.1
  183.3 1.3 fusion.15
  184.6 2.4 fusion.3
  187.7 1.3 select_n.315
  189.1 1.5 add_select_fusion.2
  190.5 2.9 fusion.14
  193.5 3.5 fusion.5
  197.7 1.4 select_n.308
  199.1 1.5 add_select_fusion.3
  200.5 2.9 fusion.13
  203.4 3.5 fusion.7
  207.0 1.3 select_n.312
  209.3 1.3 select_n.318
  211.6 1.3 select_n.324
  213.9 1.4 select_n.330
  216.0 1.3 fusion.125
  217.4 2.8 fusion.2
  222.5 1.2 fusion.123
  229.1 1.9 broadcast_select_fusion
  231.0 2.4 collective-permute-start.3
  234.7 1.6 pad_maximum_fusion.1
  236.3 4.1 copy.51
  241.6 1.2 convolution_multiply_fusion.30
  243.9 1.2 convolution_multiply_fusion.28
  245.1 52.0 %collective-permute-done.3 = f32[2,1024,256]{1,2,0:T(8,128)} collective-permute-done((f32[2,1024,256]{1,2,0:T(8,128)}, f32[2,1024,256]{1,2,0:T(8,128)}, u32[]{:S(2)}, u32[]{:S(2)}) %collective-permute-start.3) | collective-permute-done | bytes 2097184 | tf_op jit(solution)/shard_map/ppermute | solution.py:15
  297.1 2.9 select_add_fusion
  300.2 33.6 %collective-permute-start.4 = (f32[2,512,256]{1,2,0:T(8,128)S(1)}, f32[2,512,256]{1,2,0:T(8,128)S(1)}, u32[]{:S(2)}, u32[]{:S(2)}) collective-permute-start(f32[2,512,256]{1,2,0:T(8,128)S(1)} %slice_select_fusion), channel_id=1, source_target_pairs={{0,8},{4,12},{8,0},{12,4},{16,24},{20,28},{24,16},{28,20},{32,40},... | collective-permute-start | bytes 3145736 | tf_op jit(solution)/shard_map/ppermute | solution.py:15
  333.8 1.2 convolution_multiply_fusion.20
  336.0 1.2 convolution_multiply_fusion.24
  338.2 43.3 %collective-permute-done.4 = f32[2,512,256]{1,2,0:T(8,128)S(1)} collective-permute-done((f32[2,512,256]{1,2,0:T(8,128)S(1)}, f32[2,512,256]{1,2,0:T(8,128)S(1)}, u32[]{:S(2)}, u32[]{:S(2)}) %collective-permute-start.4) | collective-permute-done | bytes 1048608 | tf_op jit(solution)/shard_map/ppermute | solution.py:15
  382.9 519.0 %all-reduce.3.cloned.1.call-done = f32[2,1024,256]{2,0,1:T(2,128)} async-done(((f32[2,1024,256]{2,0,1:T(2,128)}), f32[2,1024,256]{2,0,1:T(2,128)}) %all-reduce.3.cloned.1.call-update) | async-done | bytes 2097168
  (298 shorter events, 52.3 us)
Async XLA Ops:
  7.2 93.0 %copy-start = (bf16[64,1024]{1,0:T(8,128)(2,1)S(1)}, bf16[64,1024]{1,0:T(8,128)(2,1)}, u32[]{:S(2)}) copy-start(bf16[64,1024]{1,0:T(8,128)(2,1)} %param.6) | copy-start | bytes 393220
  7.2 93.0 %all-gather.2.cloned.1.call-start = ((), (), s32[]{:S(2)}) async-start(), calls=%async_computation.2 | async-start | bytes 2621440 | tf_op jit(solution)/shard_map/all_gather | solution.py:88
  7.2 43.0 %copy-start.35 = (bf16[256,256]{1,0:T(8,128)(2,1)S(1)}, bf16[256,256]{1,0:T(8,128)(2,1)}, u32[]{:S(2)}) copy-start(bf16[256,256]{1,0:T(8,128)(2,1)} %param.9) | copy-start | bytes 393220
  8.3 42.8 %copy-start.36 = (bf16[256,256]{1,0:T(8,128)(2,1)S(1)}, bf16[256,256]{1,0:T(8,128)(2,1)}, u32[]{:S(2)}) copy-start(bf16[256,256]{1,0:T(8,128)(2,1)} %param.10) | copy-start | bytes 393220
  8.3 8.3 collective-permute-start
  10.3 41.7 %copy-start.24 = (bf16[256,256]{1,0:T(8,128)(2,1)S(1)}, bf16[256,256]{1,0:T(8,128)(2,1)}, u32[]{:S(2)}) copy-start(bf16[256,256]{1,0:T(8,128)(2,1)} %param.8) | copy-start | bytes 393220
  10.4 42.5 %copy-start.92 = (u32[256]{0:T(256)S(1)}, u32[256]{0:T(256)}, u32[]{:S(2)}) copy-start(u32[256]{0:T(256)} %constant.137) | copy-start | bytes 3076
  10.4 43.7 %copy-start.91 = (s32[16]{0:T(128)S(1)}, s32[16]{0:T(128)}, u32[]{:S(2)}) copy-start(s32[16]{0:T(128)} %param.11) | copy-start | bytes 196
  17.9 25.8 %collective-permute-start.1 = (bf16[2,512,256]{2,1,0:T(8,128)(2,1)S(1)}, bf16[2,512,256]{2,1,0:T(8,128)(2,1)S(1)}, u32[]{:S(2)}, u32[]{:S(2)}) collective-permute-start(bf16[2,512,256]{2,1,0:T(8,128)(2,1)S(1)} %maximum_select_fusion.2), channel_id=1, source_target_pairs={{0,8},{4,12},{8,0},{12,4},{16,24},{20,28},{24,16},{28,20},{32,40},... | collective-permute-start | bytes 1572872 | tf_op jit(solution)/shard_map/ppermute | solution.py:15
  44.0 52.1 %collective-permute-start.2 = (bf16[2,1024,256]{2,1,0:T(8,128)(2,1)S(1)}, bf16[2,1024,256]{2,1,0:T(8,128)(2,1)S(1)}, u32[]{:S(2)}, u32[]{:S(2)}) collective-permute-start(bf16[2,1024,256]{2,1,0:T(8,128)(2,1)S(1)} %maximum_select_fusion.1), channel_id=1, source_target_pairs={{0,16},{4,20},{8,24},{12,28},{16,0},{20,4},{24,8},{28,12},{32,48},... | collective-permute-start | bytes 3145736 | tf_op jit(solution)/shard_map/ppermute | solution.py:15
  59.5 52.3 %copy-start.43 = (pred[16,4]{1,0:T(8,128)(4,1)}, pred[16,4]{1,0:T(8,128)(4,1)S(1)}, u32[]{:S(2)}) copy-start(pred[16,4]{1,0:T(8,128)(4,1)S(1)} %iota_compare_fusion) | copy-start | bytes 196
  99.6 8.4 copy-start.64
  100.1 24.1 %copy-start.63 = (f32[256]{0:T(256)}, f32[256]{0:T(256)S(1)}, u32[]{:S(2)}) copy-start(f32[256]{0:T(256)S(1)} %get-tuple-element.199) | copy-start | bytes 3076
  103.2 7.8 all-to-all-start.1
  115.2 37.8 %all-to-all-start = ((bf16[64,2,16,256]{3,2,1,0:T(8,128)(2,1)}), bf16[64,2,16,256]{3,2,1,0:T(8,128)(2,1)}, u32[]{:S(2)}, u32[]{:S(2)}) async-start(bf16[64,2,16,256]{3,2,1,0:T(8,128)(2,1)} %stack.26), calls=%async_computation | async-start | bytes 2097152 | tf_op jit(solution)/shard_map/all_to_all | solution.py:105
  124.0 777.8 %all-reduce.3.cloned.1.call-start = ((), (), s32[]{:S(2)}) async-start(), calls=%async_computation.3 | async-start | bytes 4194304
  153.0 4.7 copy-start.9
  153.0 8.1 copy-start.90
  153.0 8.3 copy-start.34
  154.4 11.1 %copy-start.12 = (bf16[1,64,16,256]{3,2,0,1:T(8,128)(2,1)}, bf16[1,64,16,256]{3,2,0,1:T(8,128)(2,1)S(1)}, u32[]{:S(2)}) copy-start(bf16[1,64,16,256]{3,2,0,1:T(8,128)(2,1)S(1)} %get-tuple-element.119) | copy-start | bytes 1572868
  154.4 9.7 %copy-start.89 = (f32[16]{0:T(128)S(1)}, f32[16]{0:T(128)}, u32[]{:S(2)}) copy-start(f32[16]{0:T(128)} %get-tuple-element.164) | copy-start | bytes 196
  154.4 9.9 %copy-start.33 = (f32[16,2048]{1,0:T(8,128)S(1)}, f32[16,2048]{1,0:T(8,128)}, u32[]{:S(2)}) copy-start(f32[16,2048]{1,0:T(8,128)} %get-tuple-element.176) | copy-start | bytes 393220
  154.8 14.1 %copy-start.31 = (f32[16,1024]{1,0:T(8,128)}, f32[16,1024]{1,0:T(8,128)S(1)}, u32[]{:S(2)}) copy-start(f32[16,1024]{1,0:T(8,128)S(1)} %get-tuple-element.163) | copy-start | bytes 196612
  155.4 11.7 %copy-start.29 = (f32[16,1024]{1,0:T(8,128)}, f32[16,1024]{1,0:T(8,128)S(1)}, u32[]{:S(2)}) copy-start(f32[16,1024]{1,0:T(8,128)S(1)} %get-tuple-element.182) | copy-start | bytes 196612
  155.5 11.5 %copy-start.88 = (f32[16]{0:T(128)S(1)}, f32[16]{0:T(128)}, u32[]{:S(2)}) copy-start(f32[16]{0:T(128)} %get-tuple-element.160) | copy-start | bytes 196
  155.5 11.7 %copy-start.32 = (f32[16,2048]{1,0:T(8,128)S(1)}, f32[16,2048]{1,0:T(8,128)}, u32[]{:S(2)}) copy-start(f32[16,2048]{1,0:T(8,128)} %get-tuple-element.161) | copy-start | bytes 393220
  157.7 10.7 %copy-start.45 = (f32[16]{0:T(128)}, f32[16]{0:T(128)S(1)}, u32[]{:S(2)}) copy-start(f32[16]{0:T(128)S(1)} %log_add_fusion.3) | copy-start | bytes 196
  161.1 8.8 copy-start.87
  161.5 8.3 copy-start.49
  164.5 5.3 copy-start.52
  171.9 4.4 copy-start.2
  173.4 6.5 copy-start.56
  176.3 3.5 copy-start.83
  176.3 3.5 copy-start.53
  176.3 3.5 copy-start.86
  183.3 3.7 copy-start.57
  189.1 4.4 copy-start.7
  190.5 6.5 copy-start.59
  193.4 3.5 copy-start.78
  193.4 3.5 copy-start.79
  193.4 3.6 copy-start.46
  193.5 3.6 copy-start.84
  199.1 4.3 copy-start.4
  200.5 6.4 copy-start.61
  203.4 3.5 copy-start.42
  203.4 3.5 copy-start.47
  203.4 3.5 copy-start.77
  211.6 8.6 copy-start.38
  213.8 6.3 copy-start.40
  217.4 4.0 copy-start.21
  217.4 4.0 copy-start.58
  229.0 4.6 copy-start.54
  229.0 4.9 copy-start.30
  229.0 4.9 copy-start.51
  229.0 5.2 copy-start.48
  229.0 5.4 copy-start.37
  231.0 66.1 %collective-permute-start.3 = (f32[2,1024,256]{1,2,0:T(8,128)}, f32[2,1024,256]{1,2,0:T(8,128)}, u32[]{:S(2)}, u32[]{:S(2)}) collective-permute-start(f32[2,1024,256]{1,2,0:T(8,128)} %broadcast_select_fusion), channel_id=1, source_target_pairs={{0,16},{4,20},{8,24},{12,28},{16,0},{20,4},{24,8},{28,12},{32,48},... | collective-permute-start | bytes 6291464 | tf_op jit(solution)/shard_map/ppermute | solution.py:15
  300.0 33.8 %copy-start.14 = (bf16[256,2048]{0,1:T(8,128)(2,1)S(1)}, bf16[256,2048]{0,1:T(8,128)(2,1)}, u32[]{:S(2)}) copy-start(bf16[256,2048]{0,1:T(8,128)(2,1)} %copy-done.13) | copy-start | bytes 3145732
  300.0 35.0 %copy-start.16 = (bf16[256,2048]{0,1:T(8,128)(2,1)S(1)}, bf16[256,2048]{0,1:T(8,128)(2,1)}, u32[]{:S(2)}) copy-start(bf16[256,2048]{0,1:T(8,128)(2,1)} %copy-done.15) | copy-start | bytes 3145732
  300.2 35.8 %copy-start.18 = (bf16[256,2048]{0,1:T(8,128)(2,1)S(1)}, bf16[256,2048]{0,1:T(8,128)(2,1)}, u32[]{:S(2)}) copy-start(bf16[256,2048]{0,1:T(8,128)(2,1)} %copy-done.17) | copy-start | bytes 3145732
  300.2 37.0 %copy-start.20 = (bf16[256,2048]{0,1:T(8,128)(2,1)S(1)}, bf16[256,2048]{0,1:T(8,128)(2,1)}, u32[]{:S(2)}) copy-start(bf16[256,2048]{0,1:T(8,128)(2,1)} %copy-done.19) | copy-start | bytes 3145732
  300.2 81.2 %collective-permute-start.4 = (f32[2,512,256]{1,2,0:T(8,128)S(1)}, f32[2,512,256]{1,2,0:T(8,128)S(1)}, u32[]{:S(2)}, u32[]{:S(2)}) collective-permute-start(f32[2,512,256]{1,2,0:T(8,128)S(1)} %slice_select_fusion), channel_id=1, source_target_pairs={{0,8},{4,12},{8,0},{12,4},{16,24},{20,28},{24,16},{28,20},{32,40},... | collective-permute-start | bytes 3145736 | tf_op jit(solution)/shard_map/ppermute | solution.py:15
  338.2 564.7 %copy-start.44 = (pred[16,4]{1,0:T(8,128)(4,1)S(1)}, pred[16,4]{1,0:T(8,128)(4,1)}, u32[]{:S(2)}) copy-start(pred[16,4]{1,0:T(8,128)(4,1)} %copy-done.43) | copy-start | bytes 196
  382.7 523.9 %collective-permute-start.5 = (f32[2,256,256]{1,2,0:T(8,128)}, f32[2,256,256]{1,2,0:T(8,128)S(1)}, u32[]{:S(2)}, u32[]{:S(2)}) collective-permute-start(f32[2,256,256]{1,2,0:T(8,128)} %slice_select_fusion.1), channel_id=1, source_target_pairs={{0,4},{4,0},{8,12},{12,8},{16,20},{20,16},{24,28},{28,24},{32,36},... | collective-permute-start | bytes 1572872 | tf_op jit(solution)/shard_map/ppermute | solution.py:15
  (39 other events, 79.5 us)
Sparse Core Ops, SparseCore 0:
  10.5 28.7 all-gather.1
  240.6 661.2 all-reduce.2
